TPU v7x, 256 devices: a whole 4x4x8 slice. The times are simulated.
256 devices in a mesh: depth: 64 (over x, z_hi, y), freq: 4 (over z_lo, core).
Axes of the slice: x: 4, y: 4, z: 8 (z_hi: 4, z_lo: 2; z = z_hi * 2 + z_lo), core: 2. Of those that a mesh axis runs over, the one named last changes fastest.
Arguments:
- source_field: float32 [4, 2, 64, 2048], P('freq'), may hold values from -6 to 6
- receiver_data: float32 [4, 2, 64, 2048], P('freq'), may hold values from -6 to 6
- propagator: bfloat16 [4, 64, 16, 6, 2, 128, 128], P('freq', 'depth'), may hold values from -0.102062073 to 0.102062073
- block_columns: int32 [64, 16, 6], P('depth'), may hold values from 0 to 15, as said below
- image_pairs: int32 [64, 8, 2], P('depth'), may hold values from 0 to 15, as said below
Outputs:
- image: float32 [64, 8, 128, 128], P('depth', 'freq')
Inputs may be any that keep to these rules, and one draw needn't show every extreme that they name: `block_columns`: each block row lists 6 distinct block columns, its own among them. `image_pairs`: the two block indices of a pair differ by at most one.
All inputs are finite; a program needn't handle non-finite values.
Results may differ from a plain program's by a relative error of at most 0.0003.
Values sent between devices are 32-bit elements; how exact they have to be, the bound alone decides.
A program may use at most 64 MiB of HBM per device.

v0:
```python
import math

import jax
import jax.numpy as jnp
from jax import lax
from jax.sharding import PartitionSpec as P

NG = 8


def passed_along(value, axis, steps):
    count = lax.axis_size(axis)
    initial, last = (max(0, -steps), min(count, count - steps))
    return lax.ppermute(value, axis, [(source, source + steps) for source in range(initial, last)])


def edge_taper(lateral):
    position = jnp.arange(lateral, dtype=jnp.int32)
    distance = jnp.minimum(position, lateral - 1 - position).astype(jnp.float32)
    edge_cells = lateral // 32
    edge_ramp = jnp.maximum(0.0, 1.0 - distance / edge_cells)
    return 1.0 - 0.3 * edge_ramp * edge_ramp


def propagate(field, level_operator, level_columns, taper_row):
    lane_count, shot_count, lateral = field.shape
    block_rows = level_columns.shape[0]
    blocks = field.reshape(lane_count, shot_count, block_rows, lateral // block_rows)
    picked = jnp.take(blocks, level_columns, axis=2)
    operator_real = level_operator[:, :, 0].astype(jnp.float32)
    operator_imag = level_operator[:, :, 1].astype(jnp.float32)
    real_part = jnp.einsum(
        "cbrjk,rjkm->cbrm", picked, operator_real, precision=lax.Precision.HIGHEST
    )
    imag_part = jnp.einsum(
        "cbrjk,rjkm->cbrm", picked, operator_imag, precision=lax.Precision.HIGHEST
    )
    source_real = real_part[0] - imag_part[1]
    source_imag = real_part[1] + imag_part[0]
    receiver_real = real_part[2] + imag_part[3]
    receiver_imag = real_part[3] - imag_part[2]
    combined = jnp.stack([source_real, source_imag, receiver_real, receiver_imag])
    return combined.reshape(lane_count, shot_count, lateral) * taper_row


def image_level(field, level_pairs, block_size):
    lane_count, shot_count, lateral = field.shape
    blocks = field.reshape(lane_count, shot_count, lateral // block_size, block_size)
    source_blocks = jnp.take(blocks[0:2], level_pairs[:, 0], axis=2)
    receiver_blocks = jnp.take(blocks[2:4], level_pairs[:, 1], axis=2)
    return jnp.einsum(
        "csik,csim->ikm", source_blocks, receiver_blocks, precision=lax.Precision.HIGHEST
    )


def shards(source_field, receiver_data, propagator, block_columns, image_pairs):
    depth_count = lax.axis_size("depth")
    depth_index = lax.axis_index("depth")
    freq_count = lax.axis_size("freq")
    shots_all = source_field.shape[2]
    lateral = source_field.shape[3]
    levels_here = block_columns.shape[0]
    pair_count = image_pairs.shape[1]
    block_size = propagator.shape[-1]
    group_shots = shots_all // NG
    turns = depth_count + NG - 1
    taper_row = edge_taper(lateral)
    image_scale = 1.0 / math.sqrt(2.0 * shots_all * freq_count)

    def advance(field):
        field = propagate(field, propagator[0, 0], block_columns[0], taper_row)
        level_images = [image_level(field, image_pairs[0], block_size)]
        return (field, jnp.stack(level_images))

    def spare_turn(field):
        return (
            jnp.zeros_like(field),
            jnp.zeros((levels_here, pair_count, block_size, block_size), jnp.float32),
        )

    def one_turn(turn_index, loop_state):
        incoming, images = loop_state
        group_index = turn_index - depth_index
        active = jnp.logical_and(group_index >= 0, group_index < NG)
        shot_start = jnp.clip(group_index, 0, NG - 1) * group_shots

        def surface_group():
            source_part = lax.dynamic_slice_in_dim(source_field[0], shot_start, group_shots, 1)
            receiver_part = lax.dynamic_slice_in_dim(receiver_data[0], shot_start, group_shots, 1)
            return jnp.concatenate([source_part, receiver_part], axis=0)

        def from_above():
            return incoming

        entering = lax.cond(depth_index == 0, surface_group, from_above)
        leaving, fresh_images = lax.cond(active, advance, spare_turn, entering)
        passed = passed_along(leaving, "depth", 1)
        return (passed, images + fresh_images)

    initial = (
        jnp.zeros((4, group_shots, lateral), jnp.float32),
        jnp.zeros((levels_here, pair_count, block_size, block_size), jnp.float32),
    )
    unused, images = lax.fori_loop(0, turns, one_turn, initial)
    return lax.psum_scatter(images * image_scale, "freq", scatter_dimension=1, tiled=True)


def solution(mesh):
    placed = (
        P("freq", None, None, None),
        P("freq", None, None, None),
        P("freq", "depth", None, None, None, None, None),
        P("depth", None, None),
        P("depth", None, None),
    )
    return jax.shard_map(
        shards,
        mesh=mesh,
        in_specs=placed,
        out_specs=P("depth", "freq", None, None),
        check_vma=False,
    )
```

profile of v0, /device:TPU:223, one launch (start us, length us, event | category | flops | bytes accessed | tf_op | source)
XLA Modules:
  0.0 1577.4 jit_solution(17768152416266721444)
XLA Ops:
  14.7 1455.2 %while.20 = (s32[]{:T(128)}, f32[4,8,2048]{2,1,0:T(8,128)S(1)}, f32[1,8,128,128]{3,2,1,0:T(8,128)S(1)}, s32[]{:T(128)}, pred[]{:T(512)}, /*index=5*/f32[1,2,64,2...) while((s32[]{:T(128)}, f32[4,8,2048]{2,1,0:T(8,128)S(1)}, ...), condition=%wide.region_5.7_spmd.clone, body=%wide.region_0.6_spmd.clone.sunk | while | flops 1234622464 | bytes 19587604 | solution.py:104
  62.7 18.1 %collective-permute-done = f32[4,8,2048]{2,1,0:T(8,128)S(1)} collective-permute-done((f32[4,8,2048]{2,1,0:T(8,128)}, f32[4,8,2048]{2,1,0:T(8,128)S(1)}, u32[]{:S(2)}, u32[]{:S(2)}) %collective-permute-start) | collective-permute-done | bytes 262176 | tf_op jit(solution)/shard_map/while/body/eval_jaxpr/ppermute | solution.py:14
  83.0 12.6 collective-permute-done
  97.8 17.0 %collective-permute-done = f32[4,8,2048]{2,1,0:T(8,128)S(1)} collective-permute-done((f32[4,8,2048]{2,1,0:T(8,128)}, f32[4,8,2048]{2,1,0:T(8,128)S(1)}, u32[]{:S(2)}, u32[]{:S(2)}) %collective-permute-start) | collective-permute-done | bytes 262176 | tf_op jit(solution)/shard_map/while/body/eval_jaxpr/ppermute | solution.py:14
  137.6 13.0 collective-permute-done
  152.8 19.9 %collective-permute-done = f32[4,8,2048]{2,1,0:T(8,128)S(1)} collective-permute-done((f32[4,8,2048]{2,1,0:T(8,128)}, f32[4,8,2048]{2,1,0:T(8,128)S(1)}, u32[]{:S(2)}, u32[]{:S(2)}) %collective-permute-start) | collective-permute-done | bytes 262176 | tf_op jit(solution)/shard_map/while/body/eval_jaxpr/ppermute | solution.py:14
  174.9 14.5 collective-permute-done
  191.6 14.9 collective-permute-done
  208.7 14.1 collective-permute-done
  225.0 12.9 collective-permute-done
  252.9 16.7 %collective-permute-done = f32[4,8,2048]{2,1,0:T(8,128)S(1)} collective-permute-done((f32[4,8,2048]{2,1,0:T(8,128)}, f32[4,8,2048]{2,1,0:T(8,128)S(1)}, u32[]{:S(2)}, u32[]{:S(2)}) %collective-permute-start) | collective-permute-done | bytes 262176 | tf_op jit(solution)/shard_map/while/body/eval_jaxpr/ppermute | solution.py:14
  271.9 12.9 collective-permute-done
  287.0 15.4 collective-permute-done
  304.7 13.0 collective-permute-done
  319.9 13.6 collective-permute-done
  335.7 16.5 %collective-permute-done = f32[4,8,2048]{2,1,0:T(8,128)S(1)} collective-permute-done((f32[4,8,2048]{2,1,0:T(8,128)}, f32[4,8,2048]{2,1,0:T(8,128)S(1)}, u32[]{:S(2)}, u32[]{:S(2)}) %collective-permute-start) | collective-permute-done | bytes 262176 | tf_op jit(solution)/shard_map/while/body/eval_jaxpr/ppermute | solution.py:14
  354.4 12.9 collective-permute-done
  369.6 13.4 collective-permute-done
  385.2 16.8 %collective-permute-done = f32[4,8,2048]{2,1,0:T(8,128)S(1)} collective-permute-done((f32[4,8,2048]{2,1,0:T(8,128)}, f32[4,8,2048]{2,1,0:T(8,128)S(1)}, u32[]{:S(2)}, u32[]{:S(2)}) %collective-permute-start) | collective-permute-done | bytes 262176 | tf_op jit(solution)/shard_map/while/body/eval_jaxpr/ppermute | solution.py:14
  404.2 12.9 collective-permute-done
  419.3 13.4 collective-permute-done
  434.9 16.8 %collective-permute-done = f32[4,8,2048]{2,1,0:T(8,128)S(1)} collective-permute-done((f32[4,8,2048]{2,1,0:T(8,128)}, f32[4,8,2048]{2,1,0:T(8,128)S(1)}, u32[]{:S(2)}, u32[]{:S(2)}) %collective-permute-start) | collective-permute-done | bytes 262176 | tf_op jit(solution)/shard_map/while/body/eval_jaxpr/ppermute | solution.py:14
  453.9 12.9 collective-permute-done
  469.1 13.4 collective-permute-done
  484.7 16.8 %collective-permute-done = f32[4,8,2048]{2,1,0:T(8,128)S(1)} collective-permute-done((f32[4,8,2048]{2,1,0:T(8,128)}, f32[4,8,2048]{2,1,0:T(8,128)S(1)}, u32[]{:S(2)}, u32[]{:S(2)}) %collective-permute-start) | collective-permute-done | bytes 262176 | tf_op jit(solution)/shard_map/while/body/eval_jaxpr/ppermute | solution.py:14
  503.6 12.9 collective-permute-done
  518.8 13.4 collective-permute-done
  534.4 16.8 %collective-permute-done = f32[4,8,2048]{2,1,0:T(8,128)S(1)} collective-permute-done((f32[4,8,2048]{2,1,0:T(8,128)}, f32[4,8,2048]{2,1,0:T(8,128)S(1)}, u32[]{:S(2)}, u32[]{:S(2)}) %collective-permute-start) | collective-permute-done | bytes 262176 | tf_op jit(solution)/shard_map/while/body/eval_jaxpr/ppermute | solution.py:14
  553.4 12.9 collective-permute-done
  568.6 13.4 collective-permute-done
  584.2 16.8 %collective-permute-done = f32[4,8,2048]{2,1,0:T(8,128)S(1)} collective-permute-done((f32[4,8,2048]{2,1,0:T(8,128)}, f32[4,8,2048]{2,1,0:T(8,128)S(1)}, u32[]{:S(2)}, u32[]{:S(2)}) %collective-permute-start) | collective-permute-done | bytes 262176 | tf_op jit(solution)/shard_map/while/body/eval_jaxpr/ppermute | solution.py:14
  603.1 12.9 collective-permute-done
  618.3 13.4 collective-permute-done
  633.9 16.8 %collective-permute-done = f32[4,8,2048]{2,1,0:T(8,128)S(1)} collective-permute-done((f32[4,8,2048]{2,1,0:T(8,128)}, f32[4,8,2048]{2,1,0:T(8,128)S(1)}, u32[]{:S(2)}, u32[]{:S(2)}) %collective-permute-start) | collective-permute-done | bytes 262176 | tf_op jit(solution)/shard_map/while/body/eval_jaxpr/ppermute | solution.py:14
  652.9 12.9 collective-permute-done
  668.1 13.4 collective-permute-done
  683.7 16.8 %collective-permute-done = f32[4,8,2048]{2,1,0:T(8,128)S(1)} collective-permute-done((f32[4,8,2048]{2,1,0:T(8,128)}, f32[4,8,2048]{2,1,0:T(8,128)S(1)}, u32[]{:S(2)}, u32[]{:S(2)}) %collective-permute-start) | collective-permute-done | bytes 262176 | tf_op jit(solution)/shard_map/while/body/eval_jaxpr/ppermute | solution.py:14
  702.6 12.9 collective-permute-done
  729.8 17.2 %collective-permute-done = f32[4,8,2048]{2,1,0:T(8,128)S(1)} collective-permute-done((f32[4,8,2048]{2,1,0:T(8,128)}, f32[4,8,2048]{2,1,0:T(8,128)S(1)}, u32[]{:S(2)}, u32[]{:S(2)}) %collective-permute-start) | collective-permute-done | bytes 262176 | tf_op jit(solution)/shard_map/while/body/eval_jaxpr/ppermute | solution.py:14
  749.3 12.9 collective-permute-done
  764.4 15.1 collective-permute-done
  781.8 13.1 collective-permute-done
  820.3 12.1 collective-permute-done
  846.9 11.0 collective-permute-done
  860.1 11.5 collective-permute-done
  873.9 13.0 collective-permute-done
  889.1 13.2 collective-permute-done
  904.6 12.5 collective-permute-done
  952.0 258.6 %collective-permute-done = f32[4,8,2048]{2,1,0:T(8,128)S(1)} collective-permute-done((f32[4,8,2048]{2,1,0:T(8,128)}, f32[4,8,2048]{2,1,0:T(8,128)S(1)}, u32[]{:S(2)}, u32[]{:S(2)}) %collective-permute-start) | collective-permute-done | bytes 262176 | tf_op jit(solution)/shard_map/while/body/eval_jaxpr/ppermute | solution.py:14
  1210.7 11.8 conditional.7
  1223.9 39.9 %collective-permute-done = f32[4,8,2048]{2,1,0:T(8,128)S(1)} collective-permute-done((f32[4,8,2048]{2,1,0:T(8,128)}, f32[4,8,2048]{2,1,0:T(8,128)S(1)}, u32[]{:S(2)}, u32[]{:S(2)}) %collective-permute-start) | collective-permute-done | bytes 262176 | tf_op jit(solution)/shard_map/while/body/eval_jaxpr/ppermute | solution.py:14
  1263.8 11.8 conditional.7
  1277.1 37.1 %collective-permute-done = f32[4,8,2048]{2,1,0:T(8,128)S(1)} collective-permute-done((f32[4,8,2048]{2,1,0:T(8,128)}, f32[4,8,2048]{2,1,0:T(8,128)S(1)}, u32[]{:S(2)}, u32[]{:S(2)}) %collective-permute-start) | collective-permute-done | bytes 262176 | tf_op jit(solution)/shard_map/while/body/eval_jaxpr/ppermute | solution.py:14
  1314.2 11.8 conditional.7
  1336.4 11.8 conditional.7
  1349.7 16.0 %collective-permute-done = f32[4,8,2048]{2,1,0:T(8,128)S(1)} collective-permute-done((f32[4,8,2048]{2,1,0:T(8,128)}, f32[4,8,2048]{2,1,0:T(8,128)S(1)}, u32[]{:S(2)}, u32[]{:S(2)}) %collective-permute-start) | collective-permute-done | bytes 262176 | tf_op jit(solution)/shard_map/while/body/eval_jaxpr/ppermute | solution.py:14
  1365.7 11.8 conditional.7
  1379.0 16.1 %collective-permute-done = f32[4,8,2048]{2,1,0:T(8,128)S(1)} collective-permute-done((f32[4,8,2048]{2,1,0:T(8,128)}, f32[4,8,2048]{2,1,0:T(8,128)S(1)}, u32[]{:S(2)}, u32[]{:S(2)}) %collective-permute-start) | collective-permute-done | bytes 262176 | tf_op jit(solution)/shard_map/while/body/eval_jaxpr/ppermute | solution.py:14
  1395.1 11.8 conditional.7
  1408.3 15.6 collective-permute-done
  1424.0 11.8 conditional.7
  1437.2 13.5 collective-permute-done
  1450.8 11.8 conditional.7
  1470.8 99.8 %reduce-scatter.2.cloned.1.call-done = f32[1,2,128,128]{3,2,1,0:T(8,128)} async-done(((f32[1,8,128,128]{3,2,1,0:T(8,128)}), f32[1,2,128,128]{3,2,1,0:T(8,128)}) %reduce-scatter.2.cloned.1.call-update) | async-done | bytes 131088 | tf_op jit(solution)/shard_map/reduce_scatter | solution.py:105
  (645 shorter events, 441.3 us)
Async XLA Ops:
  6.5 1564.0 %reduce-scatter.2.cloned.1.call-start = ((), (), s32[]{:S(2)}) async-start(), calls=%async_computation.1 | async-start | bytes 655360 | tf_op jit(solution)/shard_map/reduce_scatter | solution.py:105
  61.2 19.5 %collective-permute-start = (f32[4,8,2048]{2,1,0:T(8,128)}, f32[4,8,2048]{2,1,0:T(8,128)S(1)}, u32[]{:S(2)}, u32[]{:S(2)}) collective-permute-start(f32[4,8,2048]{2,1,0:T(8,128)} %get-tuple-element.450), channel_id=1, source_target_pairs={{0,4},{4,8},{8,12},{12,16},{16,20},{20,24},{24,28},{28,32},{32,36}... | collective-permute-start | bytes 786440 | tf_op jit(solution)/shard_map/while/body/eval_jaxpr/ppermute | solution.py:14
  81.5 14.0 collective-permute-start
  96.3 18.4 %collective-permute-start = (f32[4,8,2048]{2,1,0:T(8,128)}, f32[4,8,2048]{2,1,0:T(8,128)S(1)}, u32[]{:S(2)}, u32[]{:S(2)}) collective-permute-start(f32[4,8,2048]{2,1,0:T(8,128)} %get-tuple-element.450), channel_id=1, source_target_pairs={{0,4},{4,8},{8,12},{12,16},{16,20},{20,24},{24,28},{28,32},{32,36}... | collective-permute-start | bytes 786440 | tf_op jit(solution)/shard_map/while/body/eval_jaxpr/ppermute | solution.py:14
  125.6 9.8 collective-permute-start
  136.1 14.4 collective-permute-start
  151.3 21.3 %collective-permute-start = (f32[4,8,2048]{2,1,0:T(8,128)}, f32[4,8,2048]{2,1,0:T(8,128)S(1)}, u32[]{:S(2)}, u32[]{:S(2)}) collective-permute-start(f32[4,8,2048]{2,1,0:T(8,128)} %get-tuple-element.450), channel_id=1, source_target_pairs={{0,4},{4,8},{8,12},{12,16},{16,20},{20,24},{24,28},{28,32},{32,36}... | collective-permute-start | bytes 786440 | tf_op jit(solution)/shard_map/while/body/eval_jaxpr/ppermute | solution.py:14
  173.4 16.0 %collective-permute-start = (f32[4,8,2048]{2,1,0:T(8,128)}, f32[4,8,2048]{2,1,0:T(8,128)S(1)}, u32[]{:S(2)}, u32[]{:S(2)}) collective-permute-start(f32[4,8,2048]{2,1,0:T(8,128)} %get-tuple-element.450), channel_id=1, source_target_pairs={{0,4},{4,8},{8,12},{12,16},{16,20},{20,24},{24,28},{28,32},{32,36}... | collective-permute-start | bytes 786440 | tf_op jit(solution)/shard_map/while/body/eval_jaxpr/ppermute | solution.py:14
  190.1 16.4 %collective-permute-start = (f32[4,8,2048]{2,1,0:T(8,128)}, f32[4,8,2048]{2,1,0:T(8,128)S(1)}, u32[]{:S(2)}, u32[]{:S(2)}) collective-permute-start(f32[4,8,2048]{2,1,0:T(8,128)} %get-tuple-element.450), channel_id=1, source_target_pairs={{0,4},{4,8},{8,12},{12,16},{16,20},{20,24},{24,28},{28,32},{32,36}... | collective-permute-start | bytes 786440 | tf_op jit(solution)/shard_map/while/body/eval_jaxpr/ppermute | solution.py:14
  207.3 15.5 collective-permute-start
  223.6 14.4 collective-permute-start
  238.7 12.0 collective-permute-start
  251.4 18.2 %collective-permute-start = (f32[4,8,2048]{2,1,0:T(8,128)}, f32[4,8,2048]{2,1,0:T(8,128)S(1)}, u32[]{:S(2)}, u32[]{:S(2)}) collective-permute-start(f32[4,8,2048]{2,1,0:T(8,128)} %get-tuple-element.450), channel_id=1, source_target_pairs={{0,4},{4,8},{8,12},{12,16},{16,20},{20,24},{24,28},{28,32},{32,36}... | collective-permute-start | bytes 786440 | tf_op jit(solution)/shard_map/while/body/eval_jaxpr/ppermute | solution.py:14
  270.4 14.4 collective-permute-start
  285.6 16.8 %collective-permute-start = (f32[4,8,2048]{2,1,0:T(8,128)}, f32[4,8,2048]{2,1,0:T(8,128)S(1)}, u32[]{:S(2)}, u32[]{:S(2)}) collective-permute-start(f32[4,8,2048]{2,1,0:T(8,128)} %get-tuple-element.450), channel_id=1, source_target_pairs={{0,4},{4,8},{8,12},{12,16},{16,20},{20,24},{24,28},{28,32},{32,36}... | collective-permute-start | bytes 786440 | tf_op jit(solution)/shard_map/while/body/eval_jaxpr/ppermute | solution.py:14
  303.2 14.4 collective-permute-start
  318.4 15.0 collective-permute-start
  334.2 18.0 %collective-permute-start = (f32[4,8,2048]{2,1,0:T(8,128)}, f32[4,8,2048]{2,1,0:T(8,128)S(1)}, u32[]{:S(2)}, u32[]{:S(2)}) collective-permute-start(f32[4,8,2048]{2,1,0:T(8,128)} %get-tuple-element.450), channel_id=1, source_target_pairs={{0,4},{4,8},{8,12},{12,16},{16,20},{20,24},{24,28},{28,32},{32,36}... | collective-permute-start | bytes 786440 | tf_op jit(solution)/shard_map/while/body/eval_jaxpr/ppermute | solution.py:14
  352.9 14.4 collective-permute-start
  368.1 14.8 collective-permute-start
  383.7 18.2 %collective-permute-start = (f32[4,8,2048]{2,1,0:T(8,128)}, f32[4,8,2048]{2,1,0:T(8,128)S(1)}, u32[]{:S(2)}, u32[]{:S(2)}) collective-permute-start(f32[4,8,2048]{2,1,0:T(8,128)} %get-tuple-element.450), channel_id=1, source_target_pairs={{0,4},{4,8},{8,12},{12,16},{16,20},{20,24},{24,28},{28,32},{32,36}... | collective-permute-start | bytes 786440 | tf_op jit(solution)/shard_map/while/body/eval_jaxpr/ppermute | solution.py:14
  402.7 14.4 collective-permute-start
  417.9 14.8 collective-permute-start
  433.4 18.2 %collective-permute-start = (f32[4,8,2048]{2,1,0:T(8,128)}, f32[4,8,2048]{2,1,0:T(8,128)S(1)}, u32[]{:S(2)}, u32[]{:S(2)}) collective-permute-start(f32[4,8,2048]{2,1,0:T(8,128)} %get-tuple-element.450), channel_id=1, source_target_pairs={{0,4},{4,8},{8,12},{12,16},{16,20},{20,24},{24,28},{28,32},{32,36}... | collective-permute-start | bytes 786440 | tf_op jit(solution)/shard_map/while/body/eval_jaxpr/ppermute | solution.py:14
  452.4 14.4 collective-permute-start
  467.6 14.8 collective-permute-start
  483.2 18.2 %collective-permute-start = (f32[4,8,2048]{2,1,0:T(8,128)}, f32[4,8,2048]{2,1,0:T(8,128)S(1)}, u32[]{:S(2)}, u32[]{:S(2)}) collective-permute-start(f32[4,8,2048]{2,1,0:T(8,128)} %get-tuple-element.450), channel_id=1, source_target_pairs={{0,4},{4,8},{8,12},{12,16},{16,20},{20,24},{24,28},{28,32},{32,36}... | collective-permute-start | bytes 786440 | tf_op jit(solution)/shard_map/while/body/eval_jaxpr/ppermute | solution.py:14
  502.2 14.4 collective-permute-start
  517.4 14.8 collective-permute-start
  532.9 18.2 %collective-permute-start = (f32[4,8,2048]{2,1,0:T(8,128)}, f32[4,8,2048]{2,1,0:T(8,128)S(1)}, u32[]{:S(2)}, u32[]{:S(2)}) collective-permute-start(f32[4,8,2048]{2,1,0:T(8,128)} %get-tuple-element.450), channel_id=1, source_target_pairs={{0,4},{4,8},{8,12},{12,16},{16,20},{20,24},{24,28},{28,32},{32,36}... | collective-permute-start | bytes 786440 | tf_op jit(solution)/shard_map/while/body/eval_jaxpr/ppermute | solution.py:14
  551.9 14.4 collective-permute-start
  567.1 14.8 collective-permute-start
  582.7 18.2 %collective-permute-start = (f32[4,8,2048]{2,1,0:T(8,128)}, f32[4,8,2048]{2,1,0:T(8,128)S(1)}, u32[]{:S(2)}, u32[]{:S(2)}) collective-permute-start(f32[4,8,2048]{2,1,0:T(8,128)} %get-tuple-element.450), channel_id=1, source_target_pairs={{0,4},{4,8},{8,12},{12,16},{16,20},{20,24},{24,28},{28,32},{32,36}... | collective-permute-start | bytes 786440 | tf_op jit(solution)/shard_map/while/body/eval_jaxpr/ppermute | solution.py:14
  601.7 14.4 collective-permute-start
  616.9 14.8 collective-permute-start
  632.4 18.2 %collective-permute-start = (f32[4,8,2048]{2,1,0:T(8,128)}, f32[4,8,2048]{2,1,0:T(8,128)S(1)}, u32[]{:S(2)}, u32[]{:S(2)}) collective-permute-start(f32[4,8,2048]{2,1,0:T(8,128)} %get-tuple-element.450), channel_id=1, source_target_pairs={{0,4},{4,8},{8,12},{12,16},{16,20},{20,24},{24,28},{28,32},{32,36}... | collective-permute-start | bytes 786440 | tf_op jit(solution)/shard_map/while/body/eval_jaxpr/ppermute | solution.py:14
  651.4 14.4 collective-permute-start
  666.6 14.8 collective-permute-start
  682.2 18.2 %collective-permute-start = (f32[4,8,2048]{2,1,0:T(8,128)}, f32[4,8,2048]{2,1,0:T(8,128)S(1)}, u32[]{:S(2)}, u32[]{:S(2)}) collective-permute-start(f32[4,8,2048]{2,1,0:T(8,128)} %get-tuple-element.450), channel_id=1, source_target_pairs={{0,4},{4,8},{8,12},{12,16},{16,20},{20,24},{24,28},{28,32},{32,36}... | collective-permute-start | bytes 786440 | tf_op jit(solution)/shard_map/while/body/eval_jaxpr/ppermute | solution.py:14
  701.2 14.4 collective-permute-start
  716.3 11.2 collective-permute-start
  728.3 18.7 %collective-permute-start = (f32[4,8,2048]{2,1,0:T(8,128)}, f32[4,8,2048]{2,1,0:T(8,128)S(1)}, u32[]{:S(2)}, u32[]{:S(2)}) collective-permute-start(f32[4,8,2048]{2,1,0:T(8,128)} %get-tuple-element.450), channel_id=1, source_target_pairs={{0,4},{4,8},{8,12},{12,16},{16,20},{20,24},{24,28},{28,32},{32,36}... | collective-permute-start | bytes 786440 | tf_op jit(solution)/shard_map/while/body/eval_jaxpr/ppermute | solution.py:14
  747.8 14.4 collective-permute-start
  763.0 16.6 %collective-permute-start = (f32[4,8,2048]{2,1,0:T(8,128)}, f32[4,8,2048]{2,1,0:T(8,128)S(1)}, u32[]{:S(2)}, u32[]{:S(2)}) collective-permute-start(f32[4,8,2048]{2,1,0:T(8,128)} %get-tuple-element.450), channel_id=1, source_target_pairs={{0,4},{4,8},{8,12},{12,16},{16,20},{20,24},{24,28},{28,32},{32,36}... | collective-permute-start | bytes 786440 | tf_op jit(solution)/shard_map/while/body/eval_jaxpr/ppermute | solution.py:14
  780.4 14.6 collective-permute-start
  795.7 12.2 collective-permute-start
  818.9 13.6 collective-permute-start
  833.2 11.4 collective-permute-start
  845.4 12.5 collective-permute-start
  858.7 13.0 collective-permute-start
  872.4 14.5 collective-permute-start
  887.7 14.7 collective-permute-start
  903.1 13.9 collective-permute-start
  917.8 9.7 collective-permute-start
  928.3 10.4 collective-permute-start
  939.4 10.3 collective-permute-start
  950.5 260.1 %collective-permute-start = (f32[4,8,2048]{2,1,0:T(8,128)}, f32[4,8,2048]{2,1,0:T(8,128)S(1)}, u32[]{:S(2)}, u32[]{:S(2)}) collective-permute-start(f32[4,8,2048]{2,1,0:T(8,128)} %get-tuple-element.450), channel_id=1, source_target_pairs={{0,4},{4,8},{8,12},{12,16},{16,20},{20,24},{24,28},{28,32},{32,36}... | collective-permute-start | bytes 786440 | tf_op jit(solution)/shard_map/while/body/eval_jaxpr/ppermute | solution.py:14
  1222.5 41.4 %collective-permute-start = (f32[4,8,2048]{2,1,0:T(8,128)}, f32[4,8,2048]{2,1,0:T(8,128)S(1)}, u32[]{:S(2)}, u32[]{:S(2)}) collective-permute-start(f32[4,8,2048]{2,1,0:T(8,128)} %get-tuple-element.450), channel_id=1, source_target_pairs={{0,4},{4,8},{8,12},{12,16},{16,20},{20,24},{24,28},{28,32},{32,36}... | collective-permute-start | bytes 786440 | tf_op jit(solution)/shard_map/while/body/eval_jaxpr/ppermute | solution.py:14
  1275.6 38.5 %collective-permute-start = (f32[4,8,2048]{2,1,0:T(8,128)}, f32[4,8,2048]{2,1,0:T(8,128)S(1)}, u32[]{:S(2)}, u32[]{:S(2)}) collective-permute-start(f32[4,8,2048]{2,1,0:T(8,128)} %get-tuple-element.450), channel_id=1, source_target_pairs={{0,4},{4,8},{8,12},{12,16},{16,20},{20,24},{24,28},{28,32},{32,36}... | collective-permute-start | bytes 786440 | tf_op jit(solution)/shard_map/while/body/eval_jaxpr/ppermute | solution.py:14
  1326.0 10.4 collective-permute-start
  1348.2 17.5 %collective-permute-start = (f32[4,8,2048]{2,1,0:T(8,128)}, f32[4,8,2048]{2,1,0:T(8,128)S(1)}, u32[]{:S(2)}, u32[]{:S(2)}) collective-permute-start(f32[4,8,2048]{2,1,0:T(8,128)} %get-tuple-element.450), channel_id=1, source_target_pairs={{0,4},{4,8},{8,12},{12,16},{16,20},{20,24},{24,28},{28,32},{32,36}... | collective-permute-start | bytes 786440 | tf_op jit(solution)/shard_map/while/body/eval_jaxpr/ppermute | solution.py:14
  1377.5 17.5 %collective-permute-start = (f32[4,8,2048]{2,1,0:T(8,128)}, f32[4,8,2048]{2,1,0:T(8,128)S(1)}, u32[]{:S(2)}, u32[]{:S(2)}) collective-permute-start(f32[4,8,2048]{2,1,0:T(8,128)} %get-tuple-element.450), channel_id=1, source_target_pairs={{0,4},{4,8},{8,12},{12,16},{16,20},{20,24},{24,28},{28,32},{32,36}... | collective-permute-start | bytes 786440 | tf_op jit(solution)/shard_map/while/body/eval_jaxpr/ppermute | solution.py:14
  1406.9 17.1 %collective-permute-start = (f32[4,8,2048]{2,1,0:T(8,128)}, f32[4,8,2048]{2,1,0:T(8,128)S(1)}, u32[]{:S(2)}, u32[]{:S(2)}) collective-permute-start(f32[4,8,2048]{2,1,0:T(8,128)} %get-tuple-element.450), channel_id=1, source_target_pairs={{0,4},{4,8},{8,12},{12,16},{16,20},{20,24},{24,28},{28,32},{32,36}... | collective-permute-start | bytes 786440 | tf_op jit(solution)/shard_map/while/body/eval_jaxpr/ppermute | solution.py:14
  1435.8 15.0 collective-permute-start
  (10 other events, 84.2 us)
Sparse Core Ops, SparseCore 0:
  1470.9 99.6 reduce-scatter.1
where the time goes:
time: 1590 us; the launch traced here: 1580 us
  waiting for transfers between devices  1310 us (82%)
  starting transfers between devices  91 us (6%)
  local copies, waits for them, and re-layouts  80.4 us (5%)
  matrix products  62.3 us (4%)
  other arithmetic  19.5 us (1%)
    ppermute x71, waiting for transfers between devices, passed_along(): lax.ppermute(value, axis, [(source, source + steps) for source in range(i...  1210 us
    reduce_scatter x1, waiting for transfers between devices, shards(): lax.psum_scatter(images * image_scale, 'freq', scatter_dimension=1, tiled...  99.8 us
    ppermute x71, starting transfers between devices, passed_along(): lax.ppermute(value, axis, [(source, source + steps) for source in range(i...  91 us
    another operation x127, local copies, waits for them, and re-layouts  47.4 us
  transfers between devices with their start and end apart: 72, of which 72 were waited for; matrix products, arithmetic and copies ran while one was open for 1% of the time, Pallas kernels for 0%

commit v1 on v0

v1 whole, which is shorter than its diff:
```python
import functools
import math

import jax
import jax.numpy as jnp
from jax import lax
from jax.experimental import pallas as pl
from jax.experimental.pallas import tpu as pltpu
from jax.sharding import PartitionSpec as P

GROUP = 2
CHUNK = 2
LANE = 128
MESH = pl.DeviceIdType.MESH


def split(value):
    high = value.astype(jnp.bfloat16)
    low = (value - high.astype(jnp.float32)).astype(jnp.bfloat16)
    return high, low


def edge_row(last_block):
    lane = lax.broadcasted_iota(jnp.int32, (1, LANE), 1)
    distance = LANE - 1 - lane if last_block else lane
    ramp = jnp.maximum(0.0, 1.0 - distance.astype(jnp.float32) / 64.0)
    return 1.0 - 0.3 * ramp * ramp


def kernel(
    levels, bands, scale,
    columns, pairs, source_hbm, receiver_hbm, operator_hbm,
    image,
    operator, surface, incoming, outgoing, pieces, partial, gathered,
    load_sem, send_sem, recv_sem, part_send_sem, part_recv_sem,
):
    level = lax.axis_index("depth")
    band = lax.axis_index("freq")
    following = lax.rem(level + 1, levels)
    preceding = lax.rem(level + levels - 1, levels)
    groups = outgoing.shape[0]
    blocks = outgoing.shape[1]
    rows = outgoing.shape[2]
    half = rows // 2
    nnz = operator.shape[1]
    own_pairs = image.shape[1]

    loads = [
        pltpu.make_async_copy(operator_hbm.at[0, 0], operator, load_sem.at[0]),
        pltpu.make_async_copy(source_hbm.at[0], surface.at[0], load_sem.at[1]),
        pltpu.make_async_copy(receiver_hbm.at[0], surface.at[1], load_sem.at[2]),
    ]
    for load in loads:
        load.start()

    barrier = pltpu.get_barrier_semaphore()
    for target in (following, preceding):
        pl.semaphore_signal(barrier, inc=1, device_id=(target, band), device_id_type=MESH)
    for step in range(1, bands):
        peer = lax.rem(band + step, bands)
        pl.semaphore_signal(barrier, inc=1, device_id=(level, peer), device_id_type=MESH)
    pl.semaphore_wait(barrier, 2 + bands - 1)
    for load in loads:
        load.wait()

    sublane = lax.broadcasted_iota(jnp.int32, (8, LANE), 0)

    @pl.when(level == 0)
    def _():
        def fill(tile, carry):
            shots = pl.ds(pl.multiple_of(tile * 8, 8), 8)
            for block in range(blocks):
                lanes = pl.ds(block * LANE, LANE)
                parts = [
                    surface[0, 0, shots, lanes],
                    surface[1, 0, shots, lanes],
                    surface[0, 1, shots, lanes],
                    surface[1, 1, shots, lanes],
                ]
                for q in range(4):
                    made = parts[0] if q == 0 else pltpu.roll(parts[0], (8 - 2 * q) % 8, 0)
                    for m in range(1, 4):
                        shift = (2 * (m - q)) % 8
                        moved = parts[m] if shift == 0 else pltpu.roll(parts[m], shift, 0)
                        made = jnp.where(sublane >= 2 * m, moved, made)
                    incoming[0, tile * 4 + q, block] = made
            return carry

        lax.fori_loop(0, groups // 4, fill, 0)

    sign = jnp.where((sublane < 2) | (sublane >= 6), -1.0, 1.0).astype(jnp.float32)
    first_edge = edge_row(False)
    last_edge = edge_row(True)
    region = level // (levels - 1)

    def to_next(index, start, size):
        return pltpu.make_async_remote_copy(
            src_ref=outgoing.at[index, pl.ds(start, size)],
            dst_ref=incoming.at[region, index, pl.ds(start, size)],
            send_sem=send_sem,
            recv_sem=recv_sem.at[region, index],
            device_id=(following, band),
            device_id_type=MESH,
        )

    def arrived(which, index):
        pltpu.make_async_copy(
            incoming.at[which, index], incoming.at[which, index], recv_sem.at[which, index]
        ).wait()

    def one_group(index, carry):
        @pl.when(level > 0)
        def _():
            arrived(0, index)

        high, low = split(incoming[0, index])
        pieces[...] = jnp.concatenate([high, low], axis=1)
        for r in range(blocks):
            left = jnp.concatenate([pieces[columns[0, r, j]] for j in range(nnz)], axis=1)
            right = jnp.concatenate(
                [operator[r, :, c].reshape(nnz * LANE, LANE) for c in range(2)], axis=1
            )
            product = jnp.dot(left, right, preferred_element_type=jnp.float32)
            product = product[:rows] + product[rows:]
            turned = pltpu.roll(product[:, LANE:], half, 0)
            value = product[:, :LANE] + sign * turned
            if r == 0:
                value = value * first_edge
            if r == blocks - 1:
                value = value * last_edge
            outgoing[index, r] = value
            if r % CHUNK == CHUNK - 1:
                to_next(index, r + 1 - CHUNK, CHUNK).start()
        return carry

    lax.fori_loop(0, groups, one_group, 0)

    is_source = lax.rem(sublane, 4) < 2
    all_rows = groups * rows

    def one_pair(index, carry):
        left = outgoing[:, pairs[0, index, 0]]
        right = outgoing[:, pairs[0, index, 1]]
        left = jnp.where(is_source[None], left, 0.0)
        right = jnp.concatenate([right[:, 2:], right[:, :2]], axis=1)
        left_high, left_low = split(left.reshape(all_rows, LANE))
        right_high, right_low = split(right.reshape(all_rows, LANE))
        left_all = jnp.concatenate([left_high, left_high, left_low], axis=0)
        right_all = jnp.concatenate([right_high, right_low, right_high], axis=0)
        term = lax.dot_general(
            left_all, right_all, (((0,), (0,)), ((), ())), preferred_element_type=jnp.float32
        )
        partial[index] = term * scale
        return carry

    lax.fori_loop(0, own_pairs * bands, one_pair, 0)

    sends = []
    for step in range(1, bands):
        peer = lax.rem(band + step, bands)
        send = pltpu.make_async_remote_copy(
            src_ref=partial.at[pl.ds(peer * own_pairs, own_pairs)],
            dst_ref=gathered.at[step - 1],
            send_sem=part_send_sem.at[step - 1],
            recv_sem=part_recv_sem.at[step - 1],
            device_id=(level, peer),
            device_id_type=MESH,
        )
        send.start()
        sends.append(send)
    for send in sends:
        send.wait_recv()
    total = partial[pl.ds(band * own_pairs, own_pairs)]
    for step in range(1, bands):
        total = total + gathered[step - 1]
    image[0] = total
    for send in sends:
        send.wait_send()
    pltpu.make_async_copy(outgoing, outgoing, send_sem).wait()

    @pl.when(level == 0)
    def _():
        def drain(index, carry):
            arrived(1, index)
            return carry

        lax.fori_loop(0, groups, drain, 0)


def shards(source_field, receiver_data, propagator, block_columns, image_pairs):
    levels = lax.axis_size("depth")
    bands = lax.axis_size("freq")
    shots, lateral = source_field.shape[2:]
    blocks, nnz = propagator.shape[2:4]
    pair_count = image_pairs.shape[1]
    own_pairs = pair_count // bands
    groups = shots // GROUP
    rows = 4 * GROUP
    scale = 1.0 / math.sqrt(2.0 * shots * bands)
    tile = (LANE, LANE)
    smem = pl.BlockSpec(memory_space=pltpu.SMEM)
    anywhere = pl.BlockSpec(memory_space=pl.ANY)
    return pl.pallas_call(
        functools.partial(kernel, levels, bands, scale),
        out_shape=jax.ShapeDtypeStruct((1, own_pairs) + tile, jnp.float32),
        in_specs=[smem, smem, anywhere, anywhere, anywhere],
        out_specs=pl.BlockSpec(memory_space=pltpu.VMEM),
        scratch_shapes=[
            pltpu.VMEM((blocks, nnz, 2) + tile, jnp.bfloat16),
            pltpu.VMEM((2, 2, shots, lateral), jnp.float32),
            pltpu.VMEM((2, groups, blocks, rows, LANE), jnp.float32),
            pltpu.VMEM((groups, blocks, rows, LANE), jnp.float32),
            pltpu.VMEM((blocks, 2 * rows, LANE), jnp.bfloat16),
            pltpu.VMEM((pair_count,) + tile, jnp.float32),
            pltpu.VMEM((bands - 1, own_pairs) + tile, jnp.float32),
            pltpu.SemaphoreType.DMA((3,)),
            pltpu.SemaphoreType.DMA,
            pltpu.SemaphoreType.DMA((2, groups)),
            pltpu.SemaphoreType.DMA((bands - 1,)),
            pltpu.SemaphoreType.DMA((bands - 1,)),
        ],
        compiler_params=pltpu.CompilerParams(
            collective_id=0, has_side_effects=True, vmem_limit_bytes=48 * 2**20
        ),
    )(block_columns, image_pairs, source_field, receiver_data, propagator)


def solution(mesh):
    placed = (
        P("freq", None, None, None),
        P("freq", None, None, None),
        P("freq", "depth", None, None, None, None, None),
        P("depth", None, None),
        P("depth", None, None),
    )
    return jax.shard_map(
        shards,
        mesh=mesh,
        in_specs=placed,
        out_specs=P("depth", "freq", None, None),
        check_vma=False,
    )
```

time: 1590 us -> 475 us (0.30)
  waiting for transfers between devices: 1310 us -> 0 us
  Pallas kernels: 0 us -> 465 us
  starting transfers between devices: 91 us -> 0 us
  local copies, waits for them, and re-layouts: 80.4 us -> 4.62 us
  matrix products: 62.3 us -> 0 us
  other arithmetic: 19.5 us -> 0 us
    ppermute x71 -> x0, waiting for transfers between devices: 1210 us -> none  [passed_along(): lax.ppermute(value, axis, [(source, source + steps) for source in range(i...]
    pallas_call x0 -> x1, Pallas kernels: none -> 465 us  [shards(): pl.pallas_call(functools.partial(kernel, levels, bands, scale), out_shape...]
    reduce_scatter x1 -> x0, waiting for transfers between devices: 99.8 us -> none  [shards(): lax.psum_scatter(images * image_scale, 'freq', scatter_dimension=1, tiled...]
    ppermute x71 -> x0, starting transfers between devices: 91 us -> none  [passed_along(): lax.ppermute(value, axis, [(source, source + steps) for source in range(i...]
    dot_general x24 -> x0, matrix products: 62.3 us -> none  [the longest x8 26.9 us: propagate(): jnp.einsum('cbrjk,rjkm->cbrm', picked, operator_real, precision=lax.Preci...]
    another operation x127 -> x0, local copies, waits for them, and re-layouts: 47.4 us -> none
  transfers between devices with their start and end apart: 72 -> 0, of which waited for: 72 -> 0; matrix products, arithmetic and copies ran while one was open for 1% -> 0% of each run, Pallas kernels for 0% -> 0%
where the time goes in v1:
time: 475 us; the launch traced here: 470 us
  Pallas kernels  465 us (98%)
    pallas_call x1, Pallas kernels, shards(): pl.pallas_call(functools.partial(kernel, levels, bands, scale), out_shape...  465 us

profile of v1, /device:TPU:223, one launch (start us, length us, event | category | flops | bytes accessed | tf_op | source)
XLA Modules:
  0.0 470.1 jit_solution(6423110867918631768)
XLA Ops:
  0.0 0.8 copy.7.pairs
  0.8 0.8 copy.6.columns
  1.5 0.0 copy-start
  1.5 1.2 copy-done
  2.7 0.0 copy-start.1
  2.7 1.2 copy-done.1
  4.0 465.5 %shard_map.55 = f32[1,2,128,128]{3,2,1,0:T(8,128)S(1)} custom-call(s32[1,16,6]{2,1,0:T(8,128)S(1)} %copy.6.columns, s32[1,8,2]{2,1,0:T(8,128)S(1)} %copy.7.pairs, f32[1,2,64,2048]{3,2,1,0:T(8,128)S(1)} %copy-done, f32[1,2,64,2048]{3,2,1,0:T(8,128)S(1)} %copy-done.1, bf16[1,1,16,6,2,128,128]{6,5,4,3,2,1,0:T(8,128)(2,1)} %operator_hbm.1), custom_call_target="tpu_custom_call" | custom-call | tf_op jit(solution)/shard_map/pallas_call | solution.py:203
  469.4 0.7 copy.9
Async XLA Ops:
  1.5 1.2 copy-start
  2.7 1.2 copy-start.1

commit v2 on v1

--- a/solution.py
+++ b/solution.py
@@ -9,7 +9,10 @@
 from jax.sharding import PartitionSpec as P
 
 GROUP = 2
-CHUNK = 2
+SPLITS = ((0, 10), (10, 16))
+RUN = 4
+PLANE = 16
+SIDES = 32
 LANE = 128
 MESH = pl.DeviceIdType.MESH
 
@@ -32,12 +35,20 @@
     columns, pairs, source_hbm, receiver_hbm, operator_hbm,
     image,
     operator, surface, incoming, outgoing, pieces, partial, gathered,
-    load_sem, send_sem, recv_sem, part_send_sem, part_recv_sem,
+    load_sem, send_sem, relay_sem, recv_sem, part_send_sem, part_recv_sem,
 ):
     level = lax.axis_index("depth")
     band = lax.axis_index("freq")
-    following = lax.rem(level + 1, levels)
-    preceding = lax.rem(level + levels - 1, levels)
+    last = level // (levels - 1)
+    side_core = lax.rem(band, 2)
+    relayed = side_core * (lax.rem(level, RUN) // (RUN - 1)) * (1 - last)
+    region = relayed + 2 * last
+    detour = PLANE - RUN + 1 + SIDES * (band // 2)
+    following = lax.rem(level + 1 + (detour - 1) * relayed, levels)
+    following = following + last * (levels - 1)
+    next_band = band + last * (1 - 2 * side_core)
+    relay_target = lax.rem(level + levels + 1 - detour, levels)
+    is_relay = (side_core == 1) & (lax.rem(level, RUN) == 0) & (level != detour - 1)
     groups = outgoing.shape[0]
     blocks = outgoing.shape[1]
     rows = outgoing.shape[2]
@@ -54,12 +65,19 @@
         load.start()
 
     barrier = pltpu.get_barrier_semaphore()
-    for target in (following, preceding):
-        pl.semaphore_signal(barrier, inc=1, device_id=(target, band), device_id_type=MESH)
+    distances = [1, detour, detour - 1]
+    for distance in distances:
+        for step in (distance, levels - distance):
+            pl.semaphore_signal(
+                barrier,
+                inc=1,
+                device_id=(lax.rem(level + step, levels), band),
+                device_id_type=MESH,
+            )
     for step in range(1, bands):
         peer = lax.rem(band + step, bands)
         pl.semaphore_signal(barrier, inc=1, device_id=(level, peer), device_id_type=MESH)
-    pl.semaphore_wait(barrier, 2 + bands - 1)
+    pl.semaphore_wait(barrier, 2 * len(distances) + bands - 1)
     for load in loads:
         load.wait()
 
@@ -91,27 +109,49 @@
     sign = jnp.where((sublane < 2) | (sublane >= 6), -1.0, 1.0).astype(jnp.float32)
     first_edge = edge_row(False)
     last_edge = edge_row(True)
-    region = level // (levels - 1)
-
-    def to_next(index, start, size):
+
+    def to_next(index, part):
+        begin, end = SPLITS[part]
         return pltpu.make_async_remote_copy(
-            src_ref=outgoing.at[index, pl.ds(start, size)],
-            dst_ref=incoming.at[region, index, pl.ds(start, size)],
+            src_ref=outgoing.at[index, pl.ds(begin, end - begin)],
+            dst_ref=incoming.at[region, index, pl.ds(begin, end - begin)],
             send_sem=send_sem,
-            recv_sem=recv_sem.at[region, index],
-            device_id=(following, band),
+            recv_sem=recv_sem.at[region, index, part],
+            device_id=(following, next_band),
             device_id_type=MESH,
         )
 
-    def arrived(which, index):
-        pltpu.make_async_copy(
-            incoming.at[which, index], incoming.at[which, index], recv_sem.at[which, index]
-        ).wait()
+    def arrived(which, index, part):
+        begin, end = SPLITS[part]
+        landed = incoming.at[which, index, pl.ds(begin, end - begin)]
+        pltpu.make_async_copy(landed, landed, recv_sem.at[which, index, part]).wait()
+
+    def pass_on():
+        def one(index, carry):
+            for part, (begin, end) in enumerate(SPLITS):
+                arrived(1, index, part)
+                pltpu.make_async_remote_copy(
+                    src_ref=incoming.at[1, index, pl.ds(begin, end - begin)],
+                    dst_ref=incoming.at[0, index, pl.ds(begin, end - begin)],
+                    send_sem=relay_sem,
+                    recv_sem=recv_sem.at[0, index, part],
+                    device_id=(relay_target, band),
+                    device_id_type=MESH,
+                ).start()
+            return carry
+
+        lax.fori_loop(0, groups, one, 0)
+        pltpu.make_async_copy(outgoing, outgoing, relay_sem).wait()
+
+    @pl.when(is_relay & (level >= detour))
+    def _():
+        pass_on()
 
     def one_group(index, carry):
         @pl.when(level > 0)
         def _():
-            arrived(0, index)
+            for part in range(len(SPLITS)):
+                arrived(0, index, part)
 
         high, low = split(incoming[0, index])
         pieces[...] = jnp.concatenate([high, low], axis=1)
@@ -129,8 +169,9 @@
             if r == blocks - 1:
                 value = value * last_edge
             outgoing[index, r] = value
-            if r % CHUNK == CHUNK - 1:
-                to_next(index, r + 1 - CHUNK, CHUNK).start()
+            for part, (begin, end) in enumerate(SPLITS):
+                if r + 1 == end:
+                    to_next(index, part).start()
         return carry
 
     lax.fori_loop(0, groups, one_group, 0)
@@ -178,10 +219,15 @@
         send.wait_send()
     pltpu.make_async_copy(outgoing, outgoing, send_sem).wait()
 
-    @pl.when(level == 0)
+    @pl.when(is_relay & (level < detour))
+    def _():
+        pass_on()
+
+    @pl.when(level == levels - 1)
     def _():
         def drain(index, carry):
-            arrived(1, index)
+            for part in range(len(SPLITS)):
+                arrived(2, index, part)
             return carry
 
         lax.fori_loop(0, groups, drain, 0)
@@ -208,14 +254,15 @@
         scratch_shapes=[
             pltpu.VMEM((blocks, nnz, 2) + tile, jnp.bfloat16),
             pltpu.VMEM((2, 2, shots, lateral), jnp.float32),
-            pltpu.VMEM((2, groups, blocks, rows, LANE), jnp.float32),
+            pltpu.VMEM((3, groups, blocks, rows, LANE), jnp.float32),
             pltpu.VMEM((groups, blocks, rows, LANE), jnp.float32),
             pltpu.VMEM((blocks, 2 * rows, LANE), jnp.bfloat16),
             pltpu.VMEM((pair_count,) + tile, jnp.float32),
             pltpu.VMEM((bands - 1, own_pairs) + tile, jnp.float32),
             pltpu.SemaphoreType.DMA((3,)),
             pltpu.SemaphoreType.DMA,
-            pltpu.SemaphoreType.DMA((2, groups)),
+            pltpu.SemaphoreType.DMA,
+            pltpu.SemaphoreType.DMA((3, groups, len(SPLITS))),
             pltpu.SemaphoreType.DMA((bands - 1,)),
             pltpu.SemaphoreType.DMA((bands - 1,)),
         ],

time: 475 us -> 377 us (0.79)
  Pallas kernels: 465 us -> 372 us
    pallas_call x1, Pallas kernels: 465 us -> 372 us  [shards(): pl.pallas_call(functools.partial(kernel, levels, bands, scale), out_shape...]
where the time goes in v2:
time: 377 us; the launch traced here: 376 us
  Pallas kernels  372 us (99%)
  local copies, waits for them, and re-layouts  4.62 us (1%)
    pallas_call x1, Pallas kernels, shards(): pl.pallas_call(functools.partial(kernel, levels, bands, scale), out_shape...  372 us

profile of v2, /device:TPU:223, one launch (start us, length us, event | category | flops | bytes accessed | tf_op | source)
XLA Modules:
  0.0 376.4 jit_solution(13007704782353156196)
XLA Ops:
  0.0 0.8 copy.7.pairs
  0.8 0.8 copy.6.columns
  1.5 0.0 copy-start
  1.5 1.2 copy-done
  2.7 0.0 copy-start.1
  2.7 1.2 copy-done.1
  4.0 371.8 %shard_map.55 = f32[1,2,128,128]{3,2,1,0:T(8,128)S(1)} custom-call(s32[1,16,6]{2,1,0:T(8,128)S(1)} %copy.6.columns, s32[1,8,2]{2,1,0:T(8,128)S(1)} %copy.7.pairs, f32[1,2,64,2048]{3,2,1,0:T(8,128)S(1)} %copy-done, f32[1,2,64,2048]{3,2,1,0:T(8,128)S(1)} %copy-done.1, bf16[1,1,16,6,2,128,128]{6,5,4,3,2,1,0:T(8,128)(2,1)} %operator_hbm.1), custom_call_target="tpu_custom_call" | custom-call | tf_op jit(solution)/shard_map/pallas_call | solution.py:249
  375.8 0.7 copy.9
Async XLA Ops:
  1.5 1.2 copy-start
  2.7 1.2 copy-start.1
